TPU v7x, 256 devices: a whole 4x4x8 slice. The times are simulated.
256 devices in a mesh: azim: 32 (over y_hi, z, core), beam: 2 (over y_lo), sweep: 4 (over x).
Axes of the slice: x: 4, y: 4 (y_hi: 2, y_lo: 2; y = y_hi * 2 + y_lo), z: 8, core: 2. Of those that a mesh axis runs over, the one named last changes fastest.
Arguments:
- features: bfloat16 [2048, 4, 4, 256], P('azim', 'sweep', 'beam'), may hold values from -16 to 16
- cotangent: bfloat16 [2048, 4, 4, 256], P('azim', 'sweep', 'beam'), may hold values from -6 to 6
- w_query: bfloat16 [256, 256], replicated
- w_key: bfloat16 [256, 256], replicated
- w_value: bfloat16 [256, 256], replicated, may hold values from -0.375 to 0.375
- w_out: bfloat16 [256, 256], replicated, may hold values from -0.375 to 0.375
- w_conv: bfloat16 [256, 27, 256], replicated, may hold values from -0.078125 to 0.078125
- sector_mask: int32 [32, 32], replicated, may hold values from 0 to 1, as said below
Outputs:
- features_grad: bfloat16 [2048, 4, 4, 256], P('azim', 'sweep', 'beam')
- weight_grads: float32 [256, 31, 256], P('azim', None, ('beam', 'sweep'))
Inputs may be any that keep to these rules, and one draw needn't show every extreme that they name: `sector_mask`: entry [i, j] is 1 where query sector i may attend to key sector j, else 0; every diagonal entry is 1.
All inputs are finite; a program needn't handle non-finite values.
Results may differ from a plain program's by a relative error of at most 0.012.
The roundings to bfloat16 on the way count: a program that leaves them out, or rounds other values in their place, can miss the bound.
Values may be sent and summed in bfloat16 or wider, within the bound.
A program may use at most 128 MiB of HBM per device.

v0:
```python
import jax
import jax.numpy as jnp
from jax import lax
from jax.sharding import PartitionSpec as P

HEADS = 8
SECTOR = 64
TAPS = 27
highest = lax.Precision.HIGHEST
masked_score = -1e30


def padded_2(block, sides, width):
    for axis, dim in sides:
        count = lax.axis_size(axis)
        forward = [(i, i + 1) for i in range(count - 1)]
        forward.append((count - 1, 0))
        backward = [(target, source) for source, target in forward]
        low = lax.ppermute(
            lax.slice_in_dim(block, block.shape[dim] - width, None, axis=dim), axis, forward
        )
        high = lax.ppermute(lax.slice_in_dim(block, 0, width, axis=dim), axis, backward)
        block = jnp.concatenate([low, block, high], axis=dim)
    return block


def sector_onehot(first_row, row_total, sectors):
    sector_of = (first_row + jnp.arange(row_total, dtype=jnp.int32)) // SECTOR
    return (sector_of[:, None] == jnp.arange(sectors, dtype=jnp.int32)[None, :]).astype(jnp.float32)


def allowed_table(sector_mask, query_first, query_total, key_first, key_total):
    sectors = sector_mask.shape[0]
    query_hot = sector_onehot(query_first, query_total, sectors)
    key_hot = sector_onehot(key_first, key_total, sectors)
    lookup = jnp.dot(jnp.dot(query_hot, sector_mask.astype(jnp.float32)), key_hot.T)
    return lookup > 0.5


def split_heads(tensor):
    return tensor.reshape(tensor.shape[:3] + (HEADS, tensor.shape[3] // HEADS))


def project(flat_rows, weight):
    return jnp.dot(flat_rows, weight, preferred_element_type=jnp.float32).astype(jnp.bfloat16)


def scores_of(queries, key_rows, allowed):
    score_scale = (queries.shape[3] // HEADS) ** (-0.5)
    raw_scores = jnp.einsum(
        "asbhe,ksbhe->sbhak",
        split_heads(queries),
        split_heads(key_rows),
        preferred_element_type=jnp.float32,
    )
    return jnp.where(allowed, raw_scores * score_scale, masked_score)


def key_side(queries, grad_attended, logsum, row_delta, key_rows, value_rows, allowed):
    score_scale = (queries.shape[3] // HEADS) ** (-0.5)
    scores = scores_of(queries, key_rows, allowed)
    weights_full = jnp.where(allowed, jnp.exp(scores - logsum[..., None]), 0.0)
    grad_prob = jnp.einsum(
        "asbhe,ksbhe->sbhak",
        split_heads(grad_attended),
        split_heads(value_rows),
        preferred_element_type=jnp.float32,
    )
    grad_score = (weights_full * (grad_prob - row_delta[..., None])).astype(jnp.bfloat16)
    grad_key = (
        jnp.einsum(
            "sbhak,asbhe->ksbhe",
            grad_score,
            split_heads(queries),
            preferred_element_type=jnp.float32,
        )
        * score_scale
    )
    grad_value = jnp.einsum(
        "sbhak,asbhe->ksbhe",
        weights_full.astype(jnp.bfloat16),
        split_heads(grad_attended),
        preferred_element_type=jnp.float32,
    )
    return (grad_key.reshape(key_rows.shape), grad_value.reshape(key_rows.shape))


def edge_factors(position, devices, length):
    lower_keep = jnp.where(position > 0, 1.0, 0.0).astype(jnp.bfloat16)
    upper_keep = jnp.where(position < devices - 1, 1.0, 0.0).astype(jnp.bfloat16)
    middle = jnp.ones((length,), jnp.bfloat16)
    return jnp.concatenate([lower_keep[None], middle, upper_keep[None]])


def gather_taps(padded, col_count, sweeps, beam_rows, direction):
    pieces = []
    for offset_one in (-1, 0, 1):
        for offset_two in (-1, 0, 1):
            for offset_three in (-1, 0, 1):
                first_at = 1 + direction * offset_one
                second_at = 1 + direction * offset_two
                third_at = 1 + direction * offset_three
                pieces.append(
                    padded[
                        first_at : first_at + col_count,
                        second_at : second_at + sweeps,
                        third_at : third_at + beam_rows,
                    ]
                )
    return jnp.stack(pieces, axis=3)


def per_device(features, cotangent, w_query, w_key, w_value, w_out, w_conv, sector_mask):
    col_count, sweeps, beam_rows, channels = features.shape
    row_count = col_count * sweeps * beam_rows
    flat_in = features.reshape(row_count, channels)
    keep_edges = (
        edge_factors(lax.axis_index("sweep"), lax.axis_size("sweep"), sweeps)[:, None, None]
        * edge_factors(lax.axis_index("beam"), lax.axis_size("beam"), beam_rows)[None, :, None]
    )
    queries = project(flat_in, w_query).reshape(features.shape)
    key_proj = project(flat_in, w_key).reshape(features.shape)
    values = project(flat_in, w_value).reshape(features.shape)
    col_first = lax.axis_index("azim") * col_count
    key_all, value_all = (
        lax.all_gather(key_proj, "azim", axis=0, tiled=True),
        lax.all_gather(values, "azim", axis=0, tiled=True),
    )
    allowed_all = allowed_table(sector_mask, col_first, col_count, 0, key_all.shape[0])
    scores = scores_of(queries, key_all, allowed_all)
    peak_score = jnp.max(scores, axis=-1)
    logsum = peak_score + jnp.log(jnp.sum(jnp.exp(scores - peak_score[..., None]), axis=-1))
    weights_full = jnp.where(allowed_all, jnp.exp(scores - logsum[..., None]), 0.0)
    attended = jnp.einsum(
        "sbhak,ksbhe->asbhe",
        weights_full.astype(jnp.bfloat16),
        split_heads(value_all),
        preferred_element_type=jnp.float32,
    )
    attended = attended.reshape(features.shape).astype(jnp.bfloat16)
    attended_flat = attended.reshape(row_count, channels)
    mixed_out = flat_in.astype(jnp.float32) + jnp.dot(
        attended_flat, w_out, preferred_element_type=jnp.float32
    )
    layer_out = mixed_out.reshape(features.shape).astype(jnp.bfloat16)
    both_pad = (
        padded_2(jnp.stack([layer_out, cotangent]), (("azim", 1), ("beam", 3), ("sweep", 2)), 1)
        * keep_edges
    )
    layer_pad = both_pad[0]
    cot_pad = both_pad[1]
    cot_flat = cotangent.reshape(row_count, channels)
    cot_taps = gather_taps(cot_pad, col_count, sweeps, beam_rows, -1).reshape(
        row_count, TAPS, channels
    )
    grad_layer = cot_flat.astype(jnp.float32) + jnp.einsum(
        "nto,ito->ni", cot_taps, w_conv, preferred_element_type=jnp.float32
    )
    layer_taps = gather_taps(layer_pad, col_count, sweeps, beam_rows, 1).reshape(
        row_count, TAPS, channels
    )
    grad_layer_bf = grad_layer.astype(jnp.bfloat16)
    grad_attended = (
        jnp.dot(grad_layer_bf, w_out.T, preferred_element_type=jnp.float32)
        .astype(jnp.bfloat16)
        .reshape(features.shape)
    )
    row_delta = jnp.einsum(
        "asbhe,asbhe->sbha",
        split_heads(grad_attended),
        split_heads(attended),
        preferred_element_type=jnp.float32,
    )
    grad_prob = jnp.einsum(
        "asbhe,ksbhe->sbhak",
        split_heads(grad_attended),
        split_heads(value_all),
        preferred_element_type=jnp.float32,
    )
    grad_score = (weights_full * (grad_prob - row_delta[..., None])).astype(jnp.bfloat16)
    score_scale = (channels // HEADS) ** (-0.5)
    grad_query = (
        jnp.einsum(
            "sbhak,ksbhe->asbhe",
            grad_score,
            split_heads(key_all),
            preferred_element_type=jnp.float32,
        )
        * score_scale
    )
    grad_query = grad_query.reshape(row_count, channels)
    allowed = allowed_table(
        sector_mask, col_first, col_count, jnp.int32(0), lax.axis_size("azim") * col_count
    )
    grad_key_part, grad_value_part = key_side(
        queries, grad_attended, logsum, row_delta, key_all, value_all, allowed
    )
    key_grads = lax.psum_scatter(
        jnp.concatenate([grad_key_part, grad_value_part], axis=3),
        "azim",
        scatter_dimension=0,
        tiled=True,
    )
    grad_key = key_grads[..., :channels]
    grad_value = key_grads[..., channels:]
    grad_key_flat = grad_key.reshape(row_count, channels)
    grad_value_flat = grad_value.reshape(row_count, channels)
    grad_in = grad_layer + jnp.dot(grad_query, w_query.astype(jnp.float32).T, precision=highest)
    grad_in = grad_in + jnp.dot(grad_key_flat, w_key.astype(jnp.float32).T, precision=highest)
    grad_in = grad_in + jnp.dot(grad_value_flat, w_value.astype(jnp.float32).T, precision=highest)
    features_grad = grad_in.astype(jnp.bfloat16).reshape(features.shape)
    flat_wide = flat_in.astype(jnp.float32)
    projection_terms = jnp.stack(
        [
            jnp.einsum("ni,no->io", flat_wide, grad_query, precision=highest),
            jnp.einsum("ni,no->io", flat_wide, grad_key_flat, precision=highest),
            jnp.einsum("ni,no->io", flat_wide, grad_value_flat, precision=highest),
            jnp.einsum(
                "ni,no->io", attended_flat, grad_layer_bf, preferred_element_type=jnp.float32
            ),
        ],
        axis=1,
    )
    conv_terms = jnp.einsum("nti,no->ito", layer_taps, cot_flat, preferred_element_type=jnp.float32)
    weight_rows = lax.psum_scatter(
        jnp.concatenate([projection_terms, conv_terms], axis=1),
        "azim",
        scatter_dimension=0,
        tiled=True,
    )
    weight_grads = lax.psum_scatter(weight_rows, ("beam", "sweep"), scatter_dimension=2, tiled=True)
    return (features_grad, weight_grads)


def solution(mesh):
    in_specs = (
        P("azim", "sweep", "beam", None),
        P("azim", "sweep", "beam", None),
        P(),
        P(),
        P(),
        P(),
        P(),
        P(),
    )
    out_specs = (P("azim", "sweep", "beam", None), P("azim", None, ("beam", "sweep")))
    return jax.shard_map(
        per_device, mesh=mesh, in_specs=in_specs, out_specs=out_specs, check_vma=False
    )
```

profile of v0, /device:TPU:32, one launch (start us, length us, event | category | flops | bytes accessed | tf_op | source)
XLA Modules:
  0.0 751.3 jit_solution(16207301087636658915)
XLA Ops:
  7.2 1.6 reshape.290
  8.9 1.7 convolution_convert_fusion.2
  12.2 1.7 convolution_convert_fusion.4
  17.0 1.7 convolution_convert_fusion.3
  18.7 1.7 reshape.293
  20.4 1.8 copy.106
  22.3 2.0 convolution_compare_fusion
  24.3 69.6 %all-gather.5.cloned.1.call-done = bf16[2048,1,2,256]{3,2,1,0:T(2,128)(2,1)} async-done(((bf16[64,1,2,256]{3,2,1,0:T(2,128)(2,1)}), bf16[2048,1,2,256]{3,2,1,0:T(2,128)(2,1)}) %all-gather.5.cloned.1.call-update) | async-done | bytes 2097168 | tf_op jit(solution)/shard_map/all_gather | solution.py:126
  94.0 6.2 copy.105
  100.2 3.4 fusion.1
  103.6 2.2 exponential_reduce_fusion
  106.9 66.8 %all-gather.3.cloned.1.call-done = bf16[2048,1,2,256]{3,2,1,0:T(2,128)(2,1)} async-done(((bf16[64,1,2,256]{3,2,1,0:T(2,128)(2,1)}), bf16[2048,1,2,256]{3,2,1,0:T(2,128)(2,1)}) %all-gather.3.cloned.1.call-update) | async-done | bytes 2097168 | tf_op jit(solution)/shard_map/all_gather | solution.py:127
  173.7 6.2 copy.103
  179.9 6.8 convolution_convert_fusion
  186.7 1.8 copy.107
  188.5 1.8 convert_element_type.105
  190.3 1.7 fusion.7
  197.4 1.5 collective-permute-done.1
  198.9 1.7 collective-permute-done
  204.3 1.7 collective-permute-done.3
  206.8 1.7 pad_maximum_fusion.1
  208.4 2.7 collective-permute-start.5
  213.9 2.0 collective-permute-done.5
  215.9 3.5 collective-permute-done.4
  248.4 1.5 copy.118
  260.5 1.5 copy.122
  305.8 1.6 constant_dynamic-update-slice_fusion.25
  334.1 2.8 fusion.5
  338.6 8.2 %fusion.28 = f32[2,8,32,2048]{3,2,1,0:T(8,128)} fusion(bf16[64,2,8,32]{0,3,2,1:T(8,128)(2,1)S(1)} %copy.137, f32[2,8,64,2048]{3,2,1,0:T(8,128)} %copy-done.2, f32[2,8,64]{2,1,0:T(8,128)S(1)} %log_add_fusion, pred[64,2048]{1,0:T(8,128)(4,1)S(1)} %copy-done.12), kind=kOutput, calls=%fused_computation.156 | convolution fusion | flops 144703488 | bytes 12783616 | tf_op jit(solution)/shard_map/sbhak,asbhe->ksbhe/dot_general | solution.py:79
  346.8 7.2 multiply_convert_fusion
  354.0 5.4 copy.142
  359.4 5.0 convolution_multiply_fusion
  364.4 5.4 copy.141
  369.8 7.9 %pad_maximum_fusion = f32[2048,1,2,512]{3,0,2,1:T(8,128)} fusion(f32[2048,1,2,256]{3,0,2,1:T(8,128)} %copy.142, f32[2048,1,2,256]{3,0,2,1:T(8,128)} %copy.141), kind=kLoop, calls=%fused_computation | loop fusion | flops 2097152 | bytes 16777216 | tf_op jit(solution)/shard_map/concatenate | solution.py:199
  379.3 3.4 fusion.3
  385.0 145.6 %reduce-scatter.6.cloned.1.call-done = f32[64,1,2,512]{3,0,2,1:T(8,128)} async-done(((f32[2048,1,2,512]{3,0,2,1:T(8,128)}), f32[64,1,2,512]{3,0,2,1:T(8,128)}) %reduce-scatter.6.cloned.1.call-update) | async-done | bytes 262160 | tf_op jit(solution)/shard_map/reduce_scatter | solution.py:198
  535.8 3.9 bitcast_dynamic-update-slice_fusion
  541.6 150.0 %reduce-scatter.8.cloned.1.call-done = f32[8,31,256]{2,0,1:T(8,128)} async-done(((f32[256,31,256]{2,0,1:T(8,128)}), f32[8,31,256]{2,0,1:T(8,128)}) %reduce-scatter.8.cloned.1.call-update) | async-done | bytes 253968 | tf_op jit(solution)/shard_map/reduce_scatter | solution.py:225
  691.6 5.2 copy.159
  696.8 4.6 reshape.318
  701.4 1.8 fusion.33
  704.0 1.6 reshape.301
  705.6 1.7 copy.144
  707.3 1.6 reshape.302
  710.3 1.9 fusion.6
  713.7 27.2 %reduce-scatter.10.cloned.1.call-done = f32[32,248]{1,0:T(8,128)} async-done(((f32[256,248]{1,0:T(8,128)}), f32[32,248]{1,0:T(8,128)}) %reduce-scatter.10.cloned.1.call-update) | async-done | bytes 31760
  740.9 1.9 reshape.319
  742.8 2.0 copy.160
  (231 shorter events, 144.1 us)
Async XLA Ops:
  7.2 327.0 %copy-start = (bf16[256,27,256]{2,0,1:T(8,128)(2,1)S(1)}, bf16[256,27,256]{2,0,1:T(8,128)(2,1)}, u32[]{:S(2)}) copy-start(bf16[256,27,256]{2,0,1:T(8,128)(2,1)} %param.14) | copy-start | bytes 10616836
  7.2 86.8 %all-gather.5.cloned.1.call-start = ((), (), s32[]{:S(2)}) async-start(), calls=%async_computation.4 | async-start | bytes 2162688 | tf_op jit(solution)/shard_map/all_gather | solution.py:126
  12.1 161.6 %all-gather.3.cloned.1.call-start = ((), (), s32[]{:S(2)}) async-start(), calls=%async_computation.3 | async-start | bytes 2162688 | tf_op jit(solution)/shard_map/all_gather | solution.py:127
  15.4 515.2 %reduce-scatter.6.cloned.1.call-start = ((), (), s32[]{:S(2)}) async-start(), calls=%async_computation.5 | async-start | bytes 8650752 | tf_op jit(solution)/shard_map/reduce_scatter | solution.py:198
  100.2 3.5 copy-start.11
  103.6 3.3 copy-start.2
  194.4 0.6 copy-start.9
  196.3 2.6 collective-permute-start.1
  197.3 3.2 collective-permute-start
  201.5 4.4 collective-permute-start.3
  202.2 4.6 collective-permute-start.2
  206.0 0.8 copy-start.20
  206.8 1.7 copy-start.21
  208.4 7.5 collective-permute-start.5
  211.1 8.2 %collective-permute-start.4 = (bf16[2,66,1,4,256]{4,1,3,2,0:T(8,128)(2,1)}, bf16[2,66,1,4,256]{4,1,3,2,0:T(8,128)(2,1)}, u32[]{:S(2)}, u32[]{:S(2)}) collective-permute-start(bf16[2,66,1,4,256]{4,1,3,2,0:T(8,128)(2,1)} %pad_maximum_fusion.1), channel_id=1, source_target_pairs={{0,1},{1,2},{2,3},{3,0},{4,5},{5,6},{6,7},{7,4},{8,9},{9,10},{10,1... | collective-permute-start | bytes 811016 | tf_op jit(solution)/shard_map/ppermute | solution.py:19
  305.7 20.8 %copy-start.22 = (bf16[128,1,256]{2,0,1:T(8,128)(2,1)S(1)}, bf16[128,1,256]{2,0,1:T(8,128)(2,1)}, u32[]{:S(2)}) copy-start(bf16[128,1,256]{2,0,1:T(8,128)(2,1)} %stack.204) | copy-start | bytes 196612
  305.7 21.5 %copy-start.23 = (bf16[128,1,256]{2,0,1:T(8,128)(2,1)S(1)}, bf16[128,1,256]{2,0,1:T(8,128)(2,1)}, u32[]{:S(2)}) copy-start(bf16[128,1,256]{2,0,1:T(8,128)(2,1)} %stack.205) | copy-start | bytes 196612
  305.7 22.1 %copy-start.24 = (bf16[128,1,256]{2,0,1:T(8,128)(2,1)S(1)}, bf16[128,1,256]{2,0,1:T(8,128)(2,1)}, u32[]{:S(2)}) copy-start(bf16[128,1,256]{2,0,1:T(8,128)(2,1)} %stack.206) | copy-start | bytes 196612
  305.7 22.7 %copy-start.25 = (bf16[128,1,256]{2,0,1:T(8,128)(2,1)S(1)}, bf16[128,1,256]{2,0,1:T(8,128)(2,1)}, u32[]{:S(2)}) copy-start(bf16[128,1,256]{2,0,1:T(8,128)(2,1)} %stack.207) | copy-start | bytes 196612
  305.7 23.3 %copy-start.26 = (bf16[128,1,256]{2,0,1:T(8,128)(2,1)S(1)}, bf16[128,1,256]{2,0,1:T(8,128)(2,1)}, u32[]{:S(2)}) copy-start(bf16[128,1,256]{2,0,1:T(8,128)(2,1)} %stack.208) | copy-start | bytes 196612
  305.7 24.0 %copy-start.27 = (bf16[128,1,256]{2,0,1:T(8,128)(2,1)S(1)}, bf16[128,1,256]{2,0,1:T(8,128)(2,1)}, u32[]{:S(2)}) copy-start(bf16[128,1,256]{2,0,1:T(8,128)(2,1)} %stack.209) | copy-start | bytes 196612
  305.7 24.6 %copy-start.28 = (bf16[128,1,256]{2,0,1:T(8,128)(2,1)S(1)}, bf16[128,1,256]{2,0,1:T(8,128)(2,1)}, u32[]{:S(2)}) copy-start(bf16[128,1,256]{2,0,1:T(8,128)(2,1)} %stack.210) | copy-start | bytes 196612
  305.7 25.2 %copy-start.29 = (bf16[128,1,256]{2,0,1:T(8,128)(2,1)S(1)}, bf16[128,1,256]{2,0,1:T(8,128)(2,1)}, u32[]{:S(2)}) copy-start(bf16[128,1,256]{2,0,1:T(8,128)(2,1)} %stack.211) | copy-start | bytes 196612
  305.7 25.9 %copy-start.30 = (bf16[128,1,256]{2,0,1:T(8,128)(2,1)S(1)}, bf16[128,1,256]{2,0,1:T(8,128)(2,1)}, u32[]{:S(2)}) copy-start(bf16[128,1,256]{2,0,1:T(8,128)(2,1)} %stack.212) | copy-start | bytes 196612
  305.7 26.5 %copy-start.31 = (bf16[128,1,256]{2,0,1:T(8,128)(2,1)S(1)}, bf16[128,1,256]{2,0,1:T(8,128)(2,1)}, u32[]{:S(2)}) copy-start(bf16[128,1,256]{2,0,1:T(8,128)(2,1)} %stack.213) | copy-start | bytes 196612
  305.8 27.1 %copy-start.32 = (bf16[128,1,256]{2,0,1:T(8,128)(2,1)S(1)}, bf16[128,1,256]{2,0,1:T(8,128)(2,1)}, u32[]{:S(2)}) copy-start(bf16[128,1,256]{2,0,1:T(8,128)(2,1)} %stack.214) | copy-start | bytes 196612
  305.8 27.7 %copy-start.33 = (bf16[128,1,256]{2,0,1:T(8,128)(2,1)S(1)}, bf16[128,1,256]{2,0,1:T(8,128)(2,1)}, u32[]{:S(2)}) copy-start(bf16[128,1,256]{2,0,1:T(8,128)(2,1)} %stack.215) | copy-start | bytes 196612
  305.8 28.4 %copy-start.17 = (f32[128,256]{1,0:T(8,128)S(1)}, f32[128,256]{1,0:T(8,128)}, u32[]{:S(2)}) copy-start(f32[128,256]{1,0:T(8,128)} %reshape.309) | copy-start | bytes 393220
  334.1 3.4 copy-start.18
  336.9 0.7 copy-start.6
  337.6 0.9 copy-start.16
  337.6 1.0 copy-start.12
  338.6 8.2 %copy-start.8 = (bf16[2048,1,2,256]{0,3,2,1:T(8,128)(2,1)S(1)}, bf16[2048,1,2,256]{0,3,2,1:T(8,128)(2,1)}, u32[]{:S(2)}) copy-start(bf16[2048,1,2,256]{0,3,2,1:T(8,128)(2,1)} %copy.103) | copy-start | bytes 6291460
  354.0 5.4 copy-start.10
  377.7 1.6 copy-start.3
  377.7 5.5 copy-start.5
  377.7 313.9 %reduce-scatter.8.cloned.1.call-start = ((), (), s32[]{:S(2)}) async-start(), calls=%async_computation.6 | async-start | bytes 8380416 | tf_op jit(solution)/shard_map/reduce_scatter | solution.py:225
  382.7 1.7 copy-start.4
  384.3 146.3 %copy-start.15 = (bf16[64,1,2,256]{3,2,1,0:T(2,128)(2,1)S(1)}, bf16[64,1,2,256]{3,2,1,0:T(2,128)(2,1)}, u32[]{:S(2)}) copy-start(bf16[64,1,2,256]{3,2,1,0:T(2,128)(2,1)} %param.8) | copy-start | bytes 196612
  384.9 150.0 %copy-start.7 = (f32[128,256]{1,0:T(8,128)S(1)}, f32[128,256]{1,0:T(8,128)}, u32[]{:S(2)}) copy-start(f32[128,256]{1,0:T(8,128)} %copy-done.6) | copy-start | bytes 393220
  384.9 149.9 %copy-start.14 = (bf16[128,256]{1,0:T(8,128)(2,1)S(1)}, bf16[128,256]{1,0:T(8,128)(2,1)}, u32[]{:S(2)}) copy-start(bf16[128,256]{1,0:T(8,128)(2,1)} %convert_element_type.105) | copy-start | bytes 196612
  385.0 150.8 %copy-start.13 = (bf16[64,1,2,256]{3,2,1,0:T(2,128)(2,1)S(1)}, bf16[64,1,2,256]{3,2,1,0:T(2,128)(2,1)}, u32[]{:S(2)}) copy-start(bf16[64,1,2,256]{3,2,1,0:T(2,128)(2,1)} %param.9) | copy-start | bytes 196612
  539.7 0.9 copy-start.19
  539.7 201.2 %reduce-scatter.10.cloned.1.call-start = ((), (), s32[]{:S(2)}) async-start(), calls=%async_computation.7 | async-start | bytes 294912
  701.4 43.3 %copy-start.1 = (bf16[256,27,256]{2,0,1:T(8,128)(2,1)S(1)}, bf16[256,27,256]{2,0,1:T(8,128)(2,1)}, u32[]{:S(2)}) copy-start(bf16[256,27,256]{2,0,1:T(8,128)(2,1)} %param.14) | copy-start | bytes 10616836
Sparse Core Ops, SparseCore 0:
  12.2 81.6 all-gather.4
  97.3 76.3 all-gather.2
  377.8 152.7 reduce-scatter.5
  539.8 151.7 reduce-scatter.7
  701.6 39.3 reduce-scatter.9
where the time goes:
time: 756 us; the launch traced here: 751 us
  waiting for transfers between devices  471 us (62%)
  local copies, waits for them, and re-layouts  185 us (24%)
  matrix products  57.8 us (8%)
  other arithmetic  17.5 us (2%)
  between operations  14.4 us (2%)
    reduce_scatter x1, waiting for transfers between devices, per_device(): lax.psum_scatter(jnp.concatenate([projection_terms, conv_terms], axis=1),...  150 us
    reduce_scatter x1, waiting for transfers between devices, per_device(): lax.psum_scatter(jnp.concatenate([grad_key_part, grad_value_part], axis=3...  146 us
    all_gather x1, waiting for transfers between devices, per_device(): lax.all_gather(key_proj, 'azim', axis=0, tiled=True)  69.6 us
    all_gather x1, waiting for transfers between devices, per_device(): lax.all_gather(values, 'azim', axis=0, tiled=True)  66.8 us
    unnamed x129, local copies, waits for them, and re-layouts  51.9 us
    slice x29, local copies, waits for them, and re-layouts, gather_taps(): padded[first_at:first_at + col_count, second_at:second_at + sweeps, third...  42.1 us
    another operation x29, local copies, waits for them, and re-layouts, gather_taps(): return jnp.stack(pieces, axis=3)  41 us
    unnamed x6, waiting for transfers between devices  27.3 us
  transfers between devices with their start and end apart: 11, of which 11 were waited for; matrix products, arithmetic and copies ran while one was open for 6% of the time, Pallas kernels for 0%

commit v1 on v0

--- a/solution.py
+++ b/solution.py
@@ -123,7 +123,15 @@
     values = project(flat_in, w_value).reshape(features.shape)
     col_first = lax.axis_index("azim") * col_count
     key_all, value_all = (
-        lax.all_gather(key_proj, "azim", axis=0, tiled=True),
+        jnp.concatenate(
+            lax.all_to_all(
+                jnp.stack([key_proj for _ in range(lax.axis_size("azim"))]),
+                "azim",
+                split_axis=0,
+                concat_axis=0,
+            ),
+            axis=0,
+        ),
         lax.all_gather(values, "azim", axis=0, tiled=True),
     )
     allowed_all = allowed_table(sector_mask, col_first, col_count, 0, key_all.shape[0])

time: 756 us -> 698 us (0.923)
  waiting for transfers between devices: 471 us -> 390 us
  starting transfers between devices: 6.08 us -> 17.6 us
  local copies, waits for them, and re-layouts: 185 us -> 195 us
    all_gather x1 -> x0, waiting for transfers between devices: 69.6 us -> none  [per_device(): lax.all_gather(key_proj, 'azim', axis=0, tiled=True)]
    all_gather x1, waiting for transfers between devices: 66.8 us -> 13.1 us  [per_device(): lax.all_gather(values, 'azim', axis=0, tiled=True)]
    all_to_all x0 -> x1, waiting for transfers between devices: none -> 43.2 us  [per_device(): lax.all_to_all(jnp.stack([key_proj for _ in range(lax.axis_size('azim'))]...]
    another operation x3 -> x9, local copies, waits for them, and re-layouts: 0.45 us -> 14.7 us
    all_to_all x0 -> x1, starting transfers between devices: none -> 11.4 us  [per_device(): lax.all_to_all(jnp.stack([key_proj for _ in range(lax.axis_size('azim'))]...]
    unnamed x6 -> x5, waiting for transfers between devices: 27.3 us -> 27.3 us
  transfers between devices with their start and end apart: 11 -> 11, of which waited for: 11 -> 11; matrix products, arithmetic and copies ran while one was open for 6% -> 8% of each run, Pallas kernels for 0% -> 0%
where the time goes in v1:
time: 698 us; the launch traced here: 693 us
  waiting for transfers between devices  390 us (56%)
  local copies, waits for them, and re-layouts  195 us (28%)
  matrix products  57.8 us (8%)
  other arithmetic  17.7 us (3%)
  starting transfers between devices  17.6 us (3%)
  between operations  14.4 us (2%)
    reduce_scatter x1, waiting for transfers between devices, per_device(): lax.psum_scatter(jnp.concatenate([projection_terms, conv_terms], axis=1),...  150 us
    reduce_scatter x1, waiting for transfers between devices, per_device(): lax.psum_scatter(jnp.concatenate([grad_key_part, grad_value_part], axis=3...  145 us
    unnamed x129, local copies, waits for them, and re-layouts  51.6 us
    all_to_all x1, waiting for transfers between devices, per_device(): lax.all_to_all(jnp.stack([key_proj for _ in range(lax.axis_size('azim'))]...  43.2 us
    slice x29, local copies, waits for them, and re-layouts, gather_taps(): padded[first_at:first_at + col_count, second_at:second_at + sweeps, third...  42.5 us
    another operation x29, local copies, waits for them, and re-layouts, gather_taps(): return jnp.stack(pieces, axis=3)  40.9 us
    unnamed x5, waiting for transfers between devices  27.3 us
  transfers between devices with their start and end apart: 11, of which 11 were waited for; matrix products, arithmetic and copies ran while one was open for 8% of the time, Pallas kernels for 0%

profile of v1, /device:TPU:32, one launch (start us, length us, event | category | flops | bytes accessed | tf_op | source)
XLA Modules:
  0.0 693.2 jit_solution(17774769650930524653)
XLA Ops:
  7.2 1.6 reshape.288
  8.8 1.7 convolution_convert_fusion.2
  12.9 1.6 stack.190
  14.5 11.4 %all-to-all-start = ((bf16[32,64,1,2,256]{4,1,3,2,0:T(8,128)(2,1)}), bf16[32,64,1,2,256]{4,1,3,2,0:T(8,128)(2,1)}, u32[]{:S(2)}, u32[]{:S(2)}) async-start(bf16[32,64,1,2,256]{4,1,3,2,0:T(8,128)(2,1)} %stack.190), calls=%async_computation | async-start | bytes 4194304 | tf_op jit(solution)/shard_map/all_to_all | solution.py:127
  26.0 1.7 convolution_convert_fusion.4
  30.8 1.7 convolution_convert_fusion.3
  32.5 1.8 reshape.291
  34.3 1.8 copy.106
  36.1 2.0 convolution_compare_fusion
  38.2 43.2 %all-to-all-done = bf16[32,64,1,2,256]{4,1,3,2,0:T(8,128)(2,1)} async-done(((bf16[32,64,1,2,256]{4,1,3,2,0:T(8,128)(2,1)}), bf16[32,64,1,2,256]{4,1,3,2,0:T(8,128)(2,1)}, u32[]{:S(2)}, u32[]{:S(2)}) %all-to-all-start) | async-done | bytes 2097184 | tf_op jit(solution)/shard_map/all_to_all | solution.py:127
  81.4 7.4 %copy.105 = bf16[32,64,1,2,256]{1,0,4,3,2:T(8,128)(2,1)} copy(bf16[32,64,1,2,256]{4,1,3,2,0:T(8,128)(2,1)} %all-to-all-done) | data formatting | bytes 4194304 | tf_op jit(solution)/shard_map/all_to_all | solution.py:127
  88.8 6.7 reshape.292
  95.6 3.5 fusion.1
  99.1 2.2 exponential_reduce_fusion
  102.4 13.1 %all-gather.2.cloned.1.call-done = bf16[2048,1,2,256]{3,2,1,0:T(2,128)(2,1)} async-done(((bf16[64,1,2,256]{3,2,1,0:T(2,128)(2,1)}), bf16[2048,1,2,256]{3,2,1,0:T(2,128)(2,1)}) %all-gather.2.cloned.1.call-update) | async-done | bytes 2097168 | tf_op jit(solution)/shard_map/all_gather | solution.py:135
  115.5 6.2 copy.103
  121.7 6.8 convolution_convert_fusion
  128.5 1.8 copy.107
  130.3 1.8 convert_element_type.105
  132.1 1.7 fusion.7
  140.7 1.7 collective-permute-done
  146.3 1.7 collective-permute-done.3
  148.8 1.7 pad_maximum_fusion.1
  150.4 2.7 collective-permute-start.5
  156.0 1.9 collective-permute-done.5
  157.9 3.5 collective-permute-done.4
  248.0 1.6 constant_dynamic-update-slice_fusion.25
  276.1 2.8 fusion.5
  280.6 8.2 %fusion.28 = f32[2,8,32,2048]{3,2,1,0:T(8,128)} fusion(bf16[64,2,8,32]{0,3,2,1:T(8,128)(2,1)S(1)} %copy.137, f32[2,8,64,2048]{3,2,1,0:T(8,128)} %copy-done.2, f32[2,8,64]{2,1,0:T(8,128)S(1)} %log_add_fusion, pred[64,2048]{1,0:T(8,128)(4,1)S(1)} %copy-done.12), kind=kOutput, calls=%fused_computation.156 | convolution fusion | flops 144703488 | bytes 12783616 | tf_op jit(solution)/shard_map/sbhak,asbhe->ksbhe/dot_general | solution.py:79
  288.8 7.2 %multiply_convert_fusion = bf16[2,8,64,2048]{3,2,1,0:T(8,128)(2,1)} fusion(f32[2,8,64,2048]{3,2,1,0:T(8,128)} %copy-done.2, bf16[64,2,8,32]{0,3,2,1:T(8,128)(2,1)S(1)} %copy.137, bf16[2048,2,8,32]{0,3,2,1:T(8,128)(2,1)S(1)} %bitcast.297, f32[2,8,64]{2,1,0:T(8,128)S(1)} %multiply_reduce_fusion, f32[2,8,64]{2,1,0:T(8,128)S(1)} %log_add_fusion, ...), kind=kOutput, calls=%fused_computation.1 | convolution fusion | flops 148897792 | bytes 14884864 | tf_op jit(solution)/shard_map/asbhe,ksbhe->sbhak/dot_general | solution.py:182
  296.0 5.4 copy.142
  301.4 5.0 convolution_multiply_fusion
  306.4 5.4 copy.141
  311.8 7.9 %pad_maximum_fusion = f32[2048,1,2,512]{3,0,2,1:T(8,128)} fusion(f32[2048,1,2,256]{3,0,2,1:T(8,128)} %copy.142, f32[2048,1,2,256]{3,0,2,1:T(8,128)} %copy.141), kind=kLoop, calls=%fused_computation | loop fusion | flops 2097152 | bytes 16777216 | tf_op jit(solution)/shard_map/concatenate | solution.py:207
  321.3 3.4 fusion.3
  327.1 145.4 %reduce-scatter.6.cloned.1.call-done = f32[64,1,2,512]{3,0,2,1:T(8,128)} async-done(((f32[2048,1,2,512]{3,0,2,1:T(8,128)}), f32[64,1,2,512]{3,0,2,1:T(8,128)}) %reduce-scatter.6.cloned.1.call-update) | async-done | bytes 262160 | tf_op jit(solution)/shard_map/reduce_scatter | solution.py:206
  477.6 3.9 bitcast_dynamic-update-slice_fusion
  483.4 150.1 %reduce-scatter.8.cloned.1.call-done = f32[8,31,256]{2,0,1:T(8,128)} async-done(((f32[256,31,256]{2,0,1:T(8,128)}), f32[8,31,256]{2,0,1:T(8,128)}) %reduce-scatter.8.cloned.1.call-update) | async-done | bytes 253968 | tf_op jit(solution)/shard_map/reduce_scatter | solution.py:233
  633.5 5.2 copy.159
  638.7 4.6 reshape.315
  643.4 1.8 fusion.33
  645.9 1.6 reshape.298
  647.6 1.7 copy.144
  649.2 1.6 reshape.299
  652.2 1.9 fusion.6
  655.6 27.3 %reduce-scatter.10.cloned.1.call-done = f32[32,248]{1,0:T(8,128)} async-done(((f32[256,248]{1,0:T(8,128)}), f32[32,248]{1,0:T(8,128)}) %reduce-scatter.10.cloned.1.call-update) | async-done | bytes 31760
  682.8 1.9 reshape.316
  684.7 2.0 copy.160
  (233 shorter events, 149.8 us)
Async XLA Ops:
  7.2 269.0 %copy-start = (bf16[256,27,256]{2,0,1:T(8,128)(2,1)S(1)}, bf16[256,27,256]{2,0,1:T(8,128)(2,1)}, u32[]{:S(2)}) copy-start(bf16[256,27,256]{2,0,1:T(8,128)(2,1)} %param.14) | copy-start | bytes 10616836
  14.5 66.9 %all-to-all-start = ((bf16[32,64,1,2,256]{4,1,3,2,0:T(8,128)(2,1)}), bf16[32,64,1,2,256]{4,1,3,2,0:T(8,128)(2,1)}, u32[]{:S(2)}, u32[]{:S(2)}) async-start(bf16[32,64,1,2,256]{4,1,3,2,0:T(8,128)(2,1)} %stack.190), calls=%async_computation | async-start | bytes 4194304 | tf_op jit(solution)/shard_map/all_to_all | solution.py:127
  25.9 89.5 %all-gather.2.cloned.1.call-start = ((), (), s32[]{:S(2)}) async-start(), calls=%async_computation.4 | async-start | bytes 2162688 | tf_op jit(solution)/shard_map/all_gather | solution.py:135
  29.3 443.2 %reduce-scatter.6.cloned.1.call-start = ((), (), s32[]{:S(2)}) async-start(), calls=%async_computation.5 | async-start | bytes 8650752 | tf_op jit(solution)/shard_map/reduce_scatter | solution.py:206
  95.6 3.5 copy-start.11
  99.1 3.3 copy-start.2
  136.2 0.6 copy-start.9
  138.1 2.6 collective-permute-start.1
  139.2 3.2 collective-permute-start
  143.4 4.6 collective-permute-start.3
  144.2 4.6 collective-permute-start.2
  148.0 0.8 copy-start.20
  148.8 1.7 copy-start.21
  150.4 7.5 %collective-permute-start.5 = (bf16[2,66,1,4,256]{4,1,3,2,0:T(8,128)(2,1)}, bf16[2,66,1,4,256]{4,1,3,2,0:T(8,128)(2,1)}, u32[]{:S(2)}, u32[]{:S(2)}) collective-permute-start(bf16[2,66,1,4,256]{4,1,3,2,0:T(8,128)(2,1)} %pad_maximum_fusion.1), channel_id=1, source_target_pairs={{1,0},{2,1},{3,2},{0,3},{5,4},{6,5},{7,6},{4,7},{9,8},{10,9},{11,1... | collective-permute-start | bytes 811016 | tf_op jit(solution)/shard_map/ppermute | solution.py:22
  153.1 8.2 %collective-permute-start.4 = (bf16[2,66,1,4,256]{4,1,3,2,0:T(8,128)(2,1)}, bf16[2,66,1,4,256]{4,1,3,2,0:T(8,128)(2,1)}, u32[]{:S(2)}, u32[]{:S(2)}) collective-permute-start(bf16[2,66,1,4,256]{4,1,3,2,0:T(8,128)(2,1)} %pad_maximum_fusion.1), channel_id=1, source_target_pairs={{0,1},{1,2},{2,3},{3,0},{4,5},{5,6},{6,7},{7,4},{8,9},{9,10},{10,1... | collective-permute-start | bytes 811016 | tf_op jit(solution)/shard_map/ppermute | solution.py:19
  247.9 20.7 %copy-start.22 = (bf16[128,1,256]{2,0,1:T(8,128)(2,1)S(1)}, bf16[128,1,256]{2,0,1:T(8,128)(2,1)}, u32[]{:S(2)}) copy-start(bf16[128,1,256]{2,0,1:T(8,128)(2,1)} %stack.208) | copy-start | bytes 196612
  247.9 21.3 %copy-start.23 = (bf16[128,1,256]{2,0,1:T(8,128)(2,1)S(1)}, bf16[128,1,256]{2,0,1:T(8,128)(2,1)}, u32[]{:S(2)}) copy-start(bf16[128,1,256]{2,0,1:T(8,128)(2,1)} %stack.209) | copy-start | bytes 196612
  247.9 21.9 %copy-start.24 = (bf16[128,1,256]{2,0,1:T(8,128)(2,1)S(1)}, bf16[128,1,256]{2,0,1:T(8,128)(2,1)}, u32[]{:S(2)}) copy-start(bf16[128,1,256]{2,0,1:T(8,128)(2,1)} %stack.210) | copy-start | bytes 196612
  247.9 22.5 %copy-start.25 = (bf16[128,1,256]{2,0,1:T(8,128)(2,1)S(1)}, bf16[128,1,256]{2,0,1:T(8,128)(2,1)}, u32[]{:S(2)}) copy-start(bf16[128,1,256]{2,0,1:T(8,128)(2,1)} %stack.211) | copy-start | bytes 196612
  247.9 23.2 %copy-start.26 = (bf16[128,1,256]{2,0,1:T(8,128)(2,1)S(1)}, bf16[128,1,256]{2,0,1:T(8,128)(2,1)}, u32[]{:S(2)}) copy-start(bf16[128,1,256]{2,0,1:T(8,128)(2,1)} %stack.212) | copy-start | bytes 196612
  248.0 23.8 %copy-start.27 = (bf16[128,1,256]{2,0,1:T(8,128)(2,1)S(1)}, bf16[128,1,256]{2,0,1:T(8,128)(2,1)}, u32[]{:S(2)}) copy-start(bf16[128,1,256]{2,0,1:T(8,128)(2,1)} %stack.213) | copy-start | bytes 196612
  248.0 24.4 %copy-start.28 = (bf16[128,1,256]{2,0,1:T(8,128)(2,1)S(1)}, bf16[128,1,256]{2,0,1:T(8,128)(2,1)}, u32[]{:S(2)}) copy-start(bf16[128,1,256]{2,0,1:T(8,128)(2,1)} %stack.214) | copy-start | bytes 196612
  248.0 25.0 %copy-start.29 = (bf16[128,1,256]{2,0,1:T(8,128)(2,1)S(1)}, bf16[128,1,256]{2,0,1:T(8,128)(2,1)}, u32[]{:S(2)}) copy-start(bf16[128,1,256]{2,0,1:T(8,128)(2,1)} %stack.215) | copy-start | bytes 196612
  248.0 25.6 %copy-start.30 = (bf16[128,1,256]{2,0,1:T(8,128)(2,1)S(1)}, bf16[128,1,256]{2,0,1:T(8,128)(2,1)}, u32[]{:S(2)}) copy-start(bf16[128,1,256]{2,0,1:T(8,128)(2,1)} %stack.216) | copy-start | bytes 196612
  248.0 26.3 %copy-start.31 = (bf16[128,1,256]{2,0,1:T(8,128)(2,1)S(1)}, bf16[128,1,256]{2,0,1:T(8,128)(2,1)}, u32[]{:S(2)}) copy-start(bf16[128,1,256]{2,0,1:T(8,128)(2,1)} %stack.217) | copy-start | bytes 196612
  248.0 26.9 %copy-start.32 = (bf16[128,1,256]{2,0,1:T(8,128)(2,1)S(1)}, bf16[128,1,256]{2,0,1:T(8,128)(2,1)}, u32[]{:S(2)}) copy-start(bf16[128,1,256]{2,0,1:T(8,128)(2,1)} %stack.218) | copy-start | bytes 196612
  248.0 27.5 %copy-start.33 = (bf16[128,1,256]{2,0,1:T(8,128)(2,1)S(1)}, bf16[128,1,256]{2,0,1:T(8,128)(2,1)}, u32[]{:S(2)}) copy-start(bf16[128,1,256]{2,0,1:T(8,128)(2,1)} %stack.219) | copy-start | bytes 196612
  248.0 28.1 %copy-start.17 = (f32[128,256]{1,0:T(8,128)S(1)}, f32[128,256]{1,0:T(8,128)}, u32[]{:S(2)}) copy-start(f32[128,256]{1,0:T(8,128)} %reshape.306) | copy-start | bytes 393220
  276.1 3.5 copy-start.18
  278.9 0.7 copy-start.6
  279.6 0.9 copy-start.16
  279.6 1.0 copy-start.12
  280.6 8.2 %copy-start.8 = (bf16[2048,1,2,256]{0,3,2,1:T(8,128)(2,1)S(1)}, bf16[2048,1,2,256]{0,3,2,1:T(8,128)(2,1)}, u32[]{:S(2)}) copy-start(bf16[2048,1,2,256]{0,3,2,1:T(8,128)(2,1)} %copy.103) | copy-start | bytes 6291460
  296.0 5.4 copy-start.10
  319.7 1.6 copy-start.3
  319.7 5.5 copy-start.5
  319.7 313.8 %reduce-scatter.8.cloned.1.call-start = ((), (), s32[]{:S(2)}) async-start(), calls=%async_computation.6 | async-start | bytes 8380416 | tf_op jit(solution)/shard_map/reduce_scatter | solution.py:233
  324.7 1.7 copy-start.4
  326.4 146.1 %copy-start.15 = (bf16[64,1,2,256]{3,2,1,0:T(2,128)(2,1)S(1)}, bf16[64,1,2,256]{3,2,1,0:T(2,128)(2,1)}, u32[]{:S(2)}) copy-start(bf16[64,1,2,256]{3,2,1,0:T(2,128)(2,1)} %param.8) | copy-start | bytes 196612
  326.9 149.7 %copy-start.7 = (f32[128,256]{1,0:T(8,128)S(1)}, f32[128,256]{1,0:T(8,128)}, u32[]{:S(2)}) copy-start(f32[128,256]{1,0:T(8,128)} %copy-done.6) | copy-start | bytes 393220
  326.9 149.7 %copy-start.14 = (bf16[128,256]{1,0:T(8,128)(2,1)S(1)}, bf16[128,256]{1,0:T(8,128)(2,1)}, u32[]{:S(2)}) copy-start(bf16[128,256]{1,0:T(8,128)(2,1)} %convert_element_type.105) | copy-start | bytes 196612
  327.1 150.5 %copy-start.13 = (bf16[64,1,2,256]{3,2,1,0:T(2,128)(2,1)S(1)}, bf16[64,1,2,256]{3,2,1,0:T(2,128)(2,1)}, u32[]{:S(2)}) copy-start(bf16[64,1,2,256]{3,2,1,0:T(2,128)(2,1)} %param.9) | copy-start | bytes 196612
  481.5 0.9 copy-start.19
  481.5 201.3 %reduce-scatter.10.cloned.1.call-start = ((), (), s32[]{:S(2)}) async-start(), calls=%async_computation.7 | async-start | bytes 294912
  643.4 43.3 %copy-start.1 = (bf16[256,27,256]{2,0,1:T(8,128)(2,1)S(1)}, bf16[256,27,256]{2,0,1:T(8,128)(2,1)}, u32[]{:S(2)}) copy-start(bf16[256,27,256]{2,0,1:T(8,128)(2,1)} %param.14) | copy-start | bytes 10616836
Sparse Core Ops, SparseCore 0:
  30.1 85.3 all-gather.1
  319.9 152.6 reduce-scatter.5
  481.7 151.8 reduce-scatter.7
  643.5 39.3 reduce-scatter.9
